TPU v7x, 512 devices: a whole 4x4x16 slice. The times are simulated.
512 devices in a mesh: group: 64 (over z, y_hi, core), tp: 8 (over x, y_lo).
Axes of the slice: x: 4, y: 4 (y_hi: 2, y_lo: 2; y = y_hi * 2 + y_lo), z: 16, core: 2. Of those that a mesh axis runs over, the one named last changes fastest.
Arguments:
- queries: bfloat16 [4096, 2048], P('group', 'tp'), may hold values from -22 to 22
- new_kv: bfloat16 [4096, 1024], P('group', 'tp'), may hold values from -6 to 6
- local_cache: bfloat16 [16384, 1024], P('group', 'tp'), may hold values from -6 to 6
- remote_pool: bfloat16 [32768, 1024], P('group', 'tp'), may hold values from -6 to 6
- page_index: int32 [64, 64], P('group'), may hold values from 0 to 63, each once within a row
- lengths: int32 [64], P('group'), may hold values from 256 to 768, as said below
- sinks: float32 [32], P('tp'), may hold values from 4 to 8
- out_weight: bfloat16 [2048, 2880], P('tp'), may hold values from -0.125 to 0.125
- residual: bfloat16 [4096, 2880], P('group', 'tp'), may hold values from -6 to 6
- norm_gain: float32 [2880], replicated, may hold values from 0.5 to 2
- routes: int32 [4096, 4], P('group'), may hold values from 0 to 31, all different within a row; in each aligned block of 64 rows (0 to 63, 64 to 127, ...) at most 10 rows name the same one
- route_weights: float32 [4096, 4], P('group'), may hold values from 0.1 to 1
- expert_gate: bfloat16 [64, 2880, 1440], P('group', None, 'tp'), may hold values from -0.109375 to 0.109375
- expert_up: bfloat16 [64, 2880, 1440], P('group', None, 'tp'), may hold values from -0.109375 to 0.109375
- expert_down: bfloat16 [64, 1440, 2880], P('group', None, 'tp'), may hold values from -0.109375 to 0.109375
Outputs:
- layer_out: bfloat16 [4096, 2880], P('group', 'tp')
Inputs may be any that keep to these rules, and one draw needn't show every extreme that they name: `lengths`: every request has at least 256 cached positions; some request has exactly 256, some exactly 768. `routes`: within the rows of one request no expert is named by more than 10 rows. `page_index`: each row is a permutation.
All inputs are finite; a program needn't handle non-finite values.
Results may differ from a plain program's by a relative error of at most 0.013.
Values may be sent and summed in bfloat16 or wider, within the bound.
A program may use at most 64 MiB of HBM per device.

v0:
```python
import jax
import jax.numpy as jnp
from jax import lax
from jax.sharding import PartitionSpec as P

HEAD = 64
THETA = 150000.0
ALPHA = 1.702
EPSILON = 1e-05


def rotate(values, positions):
    half_dim = values.shape[-1] // 2
    inverse = THETA ** (-2.0 * jnp.arange(half_dim, dtype=jnp.float32) / values.shape[-1])
    angles = positions[:, None, None] * inverse[None, None, :]
    cosine = jnp.cos(angles)
    sine_part = jnp.sin(angles)
    first_part = values[..., :half_dim]
    second_part = values[..., half_dim:]
    return jnp.concatenate(
        [
            first_part * cosine - second_part * sine_part,
            second_part * cosine + first_part * sine_part,
        ],
        axis=-1,
    )


def attend(query_rows, kv_rows, cache_kv, cache_valid, sinks, length):
    block_len = query_rows.shape[0]
    kv_heads = kv_rows.shape[1] // (2 * HEAD)
    query_heads = query_rows.shape[1] // HEAD
    group_size = query_heads // kv_heads
    positions = (length + jnp.arange(block_len, dtype=jnp.int32)).astype(jnp.float32)
    query_rot = rotate(
        query_rows.astype(jnp.float32).reshape(block_len, query_heads, HEAD), positions
    ).astype(jnp.bfloat16)
    kv_parts = kv_rows.reshape(block_len, kv_heads, 2, HEAD)
    key_rot = rotate(kv_parts[:, :, 0].astype(jnp.float32), positions).astype(jnp.bfloat16)
    cache_parts = cache_kv.reshape(cache_kv.shape[0], kv_heads, 2, HEAD)
    all_keys = jnp.concatenate([cache_parts[:, :, 0], key_rot], axis=0)
    all_values = jnp.concatenate([cache_parts[:, :, 1], kv_parts[:, :, 1]], axis=0)
    token_order = jnp.arange(block_len, dtype=jnp.int32)
    causal = token_order[None, :] <= token_order[:, None]
    allowed = jnp.concatenate(
        [jnp.broadcast_to(cache_valid[None, :], (block_len, cache_valid.shape[0])), causal], axis=1
    )
    row_allowed = jnp.repeat(allowed, group_size, axis=0)
    score_scale = HEAD ** (-0.5)
    query_block = query_rot.reshape(block_len * group_size, HEAD)
    scores = (
        jnp.dot(query_block, all_keys[:, 0].T, preferred_element_type=jnp.float32) * score_scale
    )
    scores = jnp.where(row_allowed, scores, -jnp.inf)
    sink_rows = jnp.tile(sinks, block_len)
    row_max = jnp.maximum(jnp.max(scores, axis=1), sink_rows)
    weights = jnp.exp(scores - row_max[:, None])
    denominator = jnp.sum(weights, axis=1) + jnp.exp(sink_rows - row_max)
    blended = (
        jnp.dot(weights.astype(jnp.bfloat16), all_values[:, 0], preferred_element_type=jnp.float32)
        / denominator[:, None]
    )
    outputs = blended.astype(jnp.bfloat16).reshape(block_len, group_size * HEAD)
    return outputs


def on_device(
    queries,
    new_kv,
    local_cache,
    remote_pool,
    page_index,
    lengths,
    sinks,
    out_weight,
    residual,
    norm_gain,
    routes,
    route_weights,
    expert_gate,
    expert_up,
    expert_down,
):
    groups = lax.axis_size("group")
    lane_count = remote_pool.shape[1]
    local_len = local_cache.shape[0]
    fetched = lax.all_to_all(
        remote_pool.reshape(groups, -1, lane_count),
        "group",
        split_axis=0,
        concat_axis=0,
        tiled=True,
    )
    page_len = fetched.shape[1]
    length = lengths[0]
    offsets = jnp.arange(page_len, dtype=jnp.int32)
    remote_pos = local_len + page_index[0][:, None] * page_len + offsets[None, :]
    cache_valid = jnp.concatenate(
        [jnp.ones((local_len,), jnp.bool_), (remote_pos < length).reshape(-1)]
    )
    cache_kv = jnp.concatenate([local_cache, fetched.reshape(-1, lane_count)], axis=0)
    attended = attend(queries, new_kv, cache_kv, cache_valid, sinks, length)
    width = residual.shape[1]
    start = lax.axis_index("tp") * width
    own_gain = lax.dynamic_slice_in_dim(norm_gain, start, width, 0)
    partial_sum = jnp.dot(attended, out_weight, preferred_element_type=jnp.float32)
    own_cols = lax.dynamic_slice_in_dim(partial_sum, start, width, 1) + residual.astype(jnp.float32)
    partial_sum = lax.dynamic_update_slice_in_dim(partial_sum, own_cols, start, 1)
    hidden_state = lax.psum(partial_sum, "tp")
    mean_square = jnp.mean(hidden_state * hidden_state, axis=1, keepdims=True)
    own_state = lax.dynamic_slice_in_dim(hidden_state, start, width, 1)
    normed_own = (own_state * lax.rsqrt(mean_square + EPSILON) * own_gain).astype(jnp.bfloat16)
    block_len = normed_own.shape[0]
    top_count = routes.shape[1]
    experts = groups // 2
    capacity = 5 * block_len * top_count // (4 * experts)
    member = jnp.any(
        routes[:, :, None] == jnp.arange(experts, dtype=jnp.int32)[None, None, :], axis=1
    ).astype(jnp.int32)
    slot_rank = jnp.cumsum(member, axis=0) - member
    slot_hit = member[:, :, None] * (
        slot_rank[:, :, None] == jnp.arange(capacity, dtype=jnp.int32)[None, None, :]
    ).astype(jnp.int32)
    slot_token = jnp.sum(slot_hit * jnp.arange(block_len, dtype=jnp.int32)[:, None, None], axis=0)
    slot_valid = jnp.sum(slot_hit, axis=0)
    send_own = jnp.take(normed_own, slot_token.reshape(-1), axis=0) * slot_valid.reshape(
        -1, 1
    ).astype(jnp.bfloat16)
    hidden_part = expert_gate.shape[2]
    gate_and_up = jnp.concatenate([expert_gate[0], expert_up[0]], axis=1)
    outgoing = send_own
    feature_count = outgoing.shape[1]
    outgoing = outgoing.reshape(experts, 1, capacity, feature_count)
    outgoing = jnp.broadcast_to(outgoing, (experts, 2, capacity, feature_count)).reshape(
        groups, capacity, feature_count
    )
    whole = lax.all_gather(
        lax.all_to_all(outgoing, "group", split_axis=0, concat_axis=0, tiled=True),
        "tp",
        axis=2,
        tiled=True,
    )
    sources, slot_count, features = whole.shape
    flat_rows = whole.reshape(sources * slot_count, features)
    both = jnp.dot(flat_rows, gate_and_up, preferred_element_type=jnp.float32)
    gate_val = both[:, :hidden_part]
    up_val = both[:, hidden_part:]
    active = (gate_val * jax.nn.sigmoid(ALPHA * gate_val) * (up_val + 1.0)).astype(jnp.bfloat16)
    joined = lax.all_gather(active, "tp", axis=1, tiled=True)
    result = jnp.dot(joined, expert_down[0], preferred_element_type=jnp.float32).astype(
        jnp.bfloat16
    )
    returned = result.reshape(sources, slot_count, result.shape[1])
    arrived = lax.all_to_all(returned, "group", split_axis=0, concat_axis=0, tiled=True)
    halves = arrived.reshape(experts, 2, capacity, width).astype(jnp.float32)
    summed = (halves[:, 0] + halves[:, 1]).reshape(experts * capacity, width)
    rank_at = jnp.take_along_axis(slot_rank, routes, axis=1)
    picked = jnp.take(summed, (routes * capacity + rank_at).reshape(-1), axis=0).reshape(
        block_len, top_count, width
    )
    mixing = route_weights / jnp.sum(route_weights, axis=1, keepdims=True)
    moe_out = jnp.sum(mixing[:, :, None] * picked, axis=1)
    return (own_state + moe_out).astype(jnp.bfloat16)


def solution(mesh):
    return jax.shard_map(
        on_device,
        mesh=mesh,
        in_specs=(
            P("group", "tp"),
            P("group", "tp"),
            P("group", "tp"),
            P("group", "tp"),
            P("group", None),
            P("group"),
            P("tp"),
            P("tp", None),
            P("group", "tp"),
            P(),
            P("group", None),
            P("group", None),
            P("group", None, "tp"),
            P("group", None, "tp"),
            P("group", None, "tp"),
        ),
        out_specs=P("group", "tp"),
        check_vma=False,
    )
```

profile of v0, /device:TPU:2, one launch (start us, length us, event | category | flops | bytes accessed | tf_op | source)
XLA Modules:
  0.0 590.5 jit_solution(3634151493439080288)
XLA Ops:
  6.5 18.9 %all-to-all-start = ((bf16[64,8,128]{2,1,0:T(8,128)(2,1)}), bf16[64,8,128]{2,1,0:T(8,128)(2,1)S(1)}, u32[]{:S(2)}, u32[]{:S(2)}) async-start(bf16[64,8,128]{2,1,0:T(8,128)(2,1)} %bitcast.65), calls=%async_computation | async-start | bytes 262144 | tf_op jit(solution)/shard_map/all_to_all | solution.py:87
  26.2 0.9 reshape.390
  27.0 0.8 copy.147
  27.9 0.9 copy.144
  28.8 0.1 copy.145
  29.0 0.7 add_bitcast_fusion
  29.8 0.2 broadcast_in_dim.31
  30.1 0.3 reshape.377
  30.3 0.3 copy.148
  30.7 0.1 tile.10
  30.8 0.1 fusion.31
  31.0 0.1 copy.154
  31.1 0.1 reduce_window_sum.11
  31.2 0.8 dynamic_slice.11
  32.0 0.2 multiply_cosine_fusion
  32.2 0.2 subtract_convert_fusion
  32.4 11.6 %all-to-all-done = bf16[64,8,128]{2,1,0:T(8,128)(2,1)S(1)} async-done(((bf16[64,8,128]{2,1,0:T(8,128)(2,1)}), bf16[64,8,128]{2,1,0:T(8,128)(2,1)S(1)}, u32[]{:S(2)}, u32[]{:S(2)}) %all-to-all-start) | async-done | bytes 131104 | tf_op jit(solution)/shard_map/all_to_all | solution.py:87
  44.0 0.1 concatenate.50
  44.1 0.7 slice_maximum_fusion
  44.8 0.3 copy.146
  45.1 0.4 fusion.40
  45.5 0.2 fusion.8
  45.7 0.3 copy.149
  46.0 0.3 fusion.5
  46.3 0.1 copy.152
  46.4 0.1 reshape.382
  46.6 0.6 fusion.41
  47.3 1.1 dynamic_update_slice.3
  48.4 0.9 copy-done.1
  49.4 0.4 select_reduce_fusion
  49.9 0.1 reshape.384
  50.0 0.1 copy.160
  50.1 0.1 copy.162
  50.3 78.5 %all-reduce.3.cloned.1.call-done = f32[64,2880]{1,0:T(8,128)} async-done(((f32[64,2880]{1,0:T(8,128)}), f32[64,2880]{1,0:T(8,128)}) %all-reduce.3.cloned.1.call-update) | async-done | bytes 737296 | tf_op jit(solution)/shard_map/psum | solution.py:109
  128.8 1.3 multiply_reduce_fusion
  130.1 1.0 multiply_convert_fusion
  131.1 2.0 gather_fusion
  133.2 0.1 gather.18
  133.3 0.2 select_multiply_fusion
  133.6 59.9 %all_to_all.15 = bf16[64,10,360]{2,1,0:T(8,128)(2,1)S(1)} all-to-all(bf16[64,10,360]{2,1,0:T(8,128)(2,1)S(1)} %bitcast.58), channel_id=1, replica_groups=mesh['group'=64,'tp'=8] {'group'}, dimensions={0} | all-to-all | bytes 921600 | tf_op jit(solution)/shard_map/all_to_all | solution.py:138
  193.5 2.0 copy.165
  195.5 0.2 all-gather.6.cloned.1.call-start
  195.8 231.1 %all-gather.4.cloned.1.call-done = bf16[64,10,2880]{0,1,2:T(8,128)(2,1)} async-done(((bf16[64,10,360]{0,1,2:T(8,128)(2,1)}), bf16[64,10,2880]{0,1,2:T(8,128)(2,1)}) %all-gather.4.cloned.1.call-update) | async-done | bytes 3686416 | tf_op jit(solution)/shard_map/all_gather | solution.py:137
  426.8 17.0 %copy.166 = bf16[64,10,2880]{2,1,0:T(8,128)(2,1)} copy(bf16[64,10,2880]{0,1,2:T(8,128)(2,1)} %all-gather.4.cloned.1.call-done) | data formatting | bytes 7372800 | tf_op jit(solution)/shard_map/all_gather | solution.py:137
  443.8 7.9 %reshape.386 = bf16[640,2880]{1,0:T(8,128)(2,1)} reshape(bf16[64,10,2880]{2,1,0:T(8,128)(2,1)} %copy.166) | data formatting | bytes 7372800 | tf_op jit(solution)/shard_map/reshape | solution.py:144
  451.7 4.3 fusion
  456.0 0.9 fusion.14
  456.8 55.6 %all-gather.6.cloned.1.call-done = bf16[8,180,640]{2,1,0:T(8,128)(2,1)} async-done(((bf16[1,180,640]{2,1,0:T(8,128)(2,1)}), bf16[8,180,640]{2,1,0:T(8,128)(2,1)}) %all-gather.6.cloned.1.call-update) | async-done | bytes 1843216 | tf_op jit(solution)/shard_map/all_gather | solution.py:149
  512.5 1.7 reshape.421
  514.2 3.1 convolution_convert_fusion
  517.3 1.3 copy.167
  518.5 1.1 reshape.387
  519.6 16.0 %all-to-all-start.2 = ((bf16[64,10,360]{2,1,0:T(8,128)(2,1)}), bf16[64,10,360]{2,1,0:T(8,128)(2,1)S(1)}, u32[]{:S(2)}, u32[]{:S(2)}) async-start(bf16[64,10,360]{2,1,0:T(8,128)(2,1)} %reshape.387), calls=%async_computation.2 | async-start | bytes 1572864 | tf_op jit(solution)/shard_map/all_to_all | solution.py:154
  535.7 0.1 reshape.409
  535.9 1.9 gather_fusion.2
  537.8 0.1 reshape.412
  538.1 0.1 reshape.388
  538.2 0.1 copy.157
  538.5 42.0 %all-to-all-done.2 = bf16[64,10,360]{2,1,0:T(8,128)(2,1)S(1)} async-done(((bf16[64,10,360]{2,1,0:T(8,128)(2,1)}), bf16[64,10,360]{2,1,0:T(8,128)(2,1)S(1)}, u32[]{:S(2)}, u32[]{:S(2)}) %all-to-all-start.2) | async-done | bytes 460832 | tf_op jit(solution)/shard_map/all_to_all | solution.py:154
  580.5 0.2 convert.22
  580.9 1.0 gather_fusion.1
  581.9 0.1 gather.20
  582.0 0.4 multiply_reduce_fusion.1
  582.4 1.6 add_convert_fusion.1
  (54 shorter events, 1.5 us)
Async XLA Ops:
  6.5 40.0 %copy-start = (bf16[256,2880]{0,1:T(8,128)(2,1)S(1)}, bf16[256,2880]{0,1:T(8,128)(2,1)}, u32[]{:S(2)}) copy-start(bf16[256,2880]{0,1:T(8,128)(2,1)} %param.22) | copy-start | bytes 4423684
  6.5 24.1 %copy-start.5 = (f32[4]{0:T(128)S(1)}, f32[4]{0:T(128)}, u32[]{:S(2)}) copy-start(f32[4]{0:T(128)} %param.21) | copy-start | bytes 52
  6.5 24.4 %copy-start.3 = (s32[64,4]{0,1:T(4,128)S(1)}, s32[64,4]{0,1:T(4,128)}, u32[]{:S(2)}) copy-start(s32[64,4]{0,1:T(4,128)} %param.25) | copy-start | bytes 3076
  6.5 37.4 %all-to-all-start = ((bf16[64,8,128]{2,1,0:T(8,128)(2,1)}), bf16[64,8,128]{2,1,0:T(8,128)(2,1)S(1)}, u32[]{:S(2)}, u32[]{:S(2)}) async-start(bf16[64,8,128]{2,1,0:T(8,128)(2,1)} %bitcast.65), calls=%async_computation | async-start | bytes 262144 | tf_op jit(solution)/shard_map/all_to_all | solution.py:87
  25.4 103.4 %all-reduce.3.cloned.1.call-start = ((), (), s32[]{:S(2)}) async-start(), calls=%async_computation.3 | async-start | bytes 1507328 | tf_op jit(solution)/shard_map/psum | solution.py:109
  46.0 1.1 copy-start.2
  48.4 0.9 copy-start.1
  49.3 377.6 %all-gather.4.cloned.1.call-start = ((), (), s32[]{:S(2)}) async-start(), calls=%async_computation.4 | async-start | bytes 13271040 | tf_op jit(solution)/shard_map/all_gather | solution.py:137
  195.5 316.9 %all-gather.6.cloned.1.call-start = ((), (), s32[]{:S(2)}) async-start(), calls=%async_computation.5 | async-start | bytes 2119680 | tf_op jit(solution)/shard_map/all_gather | solution.py:149
  443.8 7.9 %copy-start.6 = (bf16[1,2880,180]{1,2,0:T(8,128)(2,1)S(1)}, bf16[1,2880,180]{1,2,0:T(8,128)(2,1)}, u32[]{:S(2)}) copy-start(bf16[1,2880,180]{1,2,0:T(8,128)(2,1)} %param.28) | copy-start | bytes 3110404
  519.6 60.9 %all-to-all-start.2 = ((bf16[64,10,360]{2,1,0:T(8,128)(2,1)}), bf16[64,10,360]{2,1,0:T(8,128)(2,1)S(1)}, u32[]{:S(2)}, u32[]{:S(2)}) async-start(bf16[64,10,360]{2,1,0:T(8,128)(2,1)} %reshape.387), calls=%async_computation.2 | async-start | bytes 1572864 | tf_op jit(solution)/shard_map/all_to_all | solution.py:154
  535.8 2.5 copy-start.4
Sparse Core Ops, SparseCore 0:
  49.4 79.3 all-reduce.2
  195.7 231.1 all-gather.3
  457.0 55.4 all-gather.5
where the time goes:
time: 592 us; the launch traced here: 591 us
  waiting for transfers between devices  419 us (71%)
  blocking collectives  59.9 us (10%)
  local copies, waits for them, and re-layouts  45.1 us (8%)
  starting transfers between devices  35.2 us (6%)
  between operations  14.2 us (2%)
  matrix products  8.63 us (1%)
  other arithmetic  8.61 us (1%)
    all_gather x1, waiting for transfers between devices, on_device(): lax.all_gather(lax.all_to_all(outgoing, 'group', split_axis=0, concat_axi...  231 us
    psum x1, waiting for transfers between devices, on_device(): hidden_state = lax.psum(partial_sum, 'tp')  78.5 us
    all_to_all x1, blocking collectives, on_device(): lax.all_to_all(outgoing, 'group', split_axis=0, concat_axis=0, tiled=True)  59.9 us
    all_gather x1, waiting for transfers between devices, on_device(): joined = lax.all_gather(active, 'tp', axis=1, tiled=True)  55.6 us
    all_to_all x1, waiting for transfers between devices, on_device(): lax.all_to_all(returned, 'group', split_axis=0, concat_axis=0, tiled=True)  42 us
    all_to_all x1, starting transfers between devices, on_device(): lax.all_to_all(remote_pool.reshape(groups, -1, lane_count), 'group', spli...  18.9 us
    all_gather x1, local copies, waits for them, and re-layouts, on_device(): lax.all_gather(lax.all_to_all(outgoing, 'group', split_axis=0, concat_axi...  17 us
    all_to_all x1, starting transfers between devices, on_device(): lax.all_to_all(returned, 'group', split_axis=0, concat_axis=0, tiled=True)  16 us
  transfers between devices with their start and end apart: 5, of which 5 were waited for; matrix products, arithmetic and copies ran while one was open for 2% of the time, Pallas kernels for 0%

commit v1 on v0

--- a/solution.py
+++ b/solution.py
@@ -106,7 +106,8 @@
     partial_sum = jnp.dot(attended, out_weight, preferred_element_type=jnp.float32)
     own_cols = lax.dynamic_slice_in_dim(partial_sum, start, width, 1) + residual.astype(jnp.float32)
     partial_sum = lax.dynamic_update_slice_in_dim(partial_sum, own_cols, start, 1)
-    hidden_state = lax.psum(partial_sum, "tp")
+    parts = lax.all_gather(partial_sum, "tp", axis=0, tiled=False)
+    hidden_state = parts.sum(axis=0)
     mean_square = jnp.mean(hidden_state * hidden_state, axis=1, keepdims=True)
     own_state = lax.dynamic_slice_in_dim(hidden_state, start, width, 1)
     normed_own = (own_state * lax.rsqrt(mean_square + EPSILON) * own_gain).astype(jnp.bfloat16)

time: 592 us -> 634 us (1.071)
  waiting for transfers between devices: 419 us -> 461 us
    all_gather x0 -> x1, waiting for transfers between devices: none -> 119 us  [on_device(): parts = lax.all_gather(partial_sum, 'tp', axis=0, tiled=False)]
    psum x1 -> x0, waiting for transfers between devices: 78.5 us -> none  [on_device(): hidden_state = lax.psum(partial_sum, 'tp')]
where the time goes in v1:
time: 634 us; the launch traced here: 633 us
  waiting for transfers between devices  461 us (73%)
  blocking collectives  60.1 us (9%)
  local copies, waits for them, and re-layouts  44.9 us (7%)
  starting transfers between devices  35.2 us (6%)
  between operations  14.2 us (2%)
  other arithmetic  8.77 us (1%)
  matrix products  8.73 us (1%)
    all_gather x1, waiting for transfers between devices, on_device(): lax.all_gather(lax.all_to_all(outgoing, 'group', split_axis=0, concat_axi...  231 us
    all_gather x1, waiting for transfers between devices, on_device(): parts = lax.all_gather(partial_sum, 'tp', axis=0, tiled=False)  119 us
    all_to_all x1, blocking collectives, on_device(): lax.all_to_all(outgoing, 'group', split_axis=0, concat_axis=0, tiled=True)  60.1 us
    all_gather x1, waiting for transfers between devices, on_device(): joined = lax.all_gather(active, 'tp', axis=1, tiled=True)  55.6 us
    all_to_all x1, waiting for transfers between devices, on_device(): lax.all_to_all(returned, 'group', split_axis=0, concat_axis=0, tiled=True)  42 us
    all_to_all x1, starting transfers between devices, on_device(): lax.all_to_all(remote_pool.reshape(groups, -1, lane_count), 'group', spli...  18.9 us
    all_gather x1, local copies, waits for them, and re-layouts, on_device(): lax.all_gather(lax.all_to_all(outgoing, 'group', split_axis=0, concat_axi...  17 us
    all_to_all x1, starting transfers between devices, on_device(): lax.all_to_all(returned, 'group', split_axis=0, concat_axis=0, tiled=True)  16 us
  transfers between devices with their start and end apart: 5, of which 5 were waited for; matrix products, arithmetic and copies ran while one was open for 2% of the time, Pallas kernels for 0%

profile of v1, /device:TPU:2, one launch (start us, length us, event | category | flops | bytes accessed | tf_op | source)
XLA Modules:
  0.0 632.8 jit_solution(13894647310669202136)
XLA Ops:
  6.5 18.9 %all-to-all-start = ((bf16[64,8,128]{2,1,0:T(8,128)(2,1)}), bf16[64,8,128]{2,1,0:T(8,128)(2,1)S(1)}, u32[]{:S(2)}, u32[]{:S(2)}) async-start(bf16[64,8,128]{2,1,0:T(8,128)(2,1)} %bitcast.69), calls=%async_computation | async-start | bytes 262144 | tf_op jit(solution)/shard_map/all_to_all | solution.py:87
  26.1 0.8 copy.147
  27.0 0.7 add_bitcast_fusion.1
  27.9 0.1 fusion.31
  28.0 0.9 reshape.392
  28.9 0.9 copy.144
  29.9 0.1 copy.145
  30.0 0.2 broadcast_in_dim.31
  30.2 0.3 reshape.379
  30.5 0.3 copy.148
  30.8 0.1 tile.10
  30.9 0.2 multiply_cosine_fusion
  31.1 0.2 subtract_convert_fusion
  31.3 12.6 %all-to-all-done = bf16[64,8,128]{2,1,0:T(8,128)(2,1)S(1)} async-done(((bf16[64,8,128]{2,1,0:T(8,128)(2,1)}), bf16[64,8,128]{2,1,0:T(8,128)(2,1)S(1)}, u32[]{:S(2)}, u32[]{:S(2)}) %all-to-all-start) | async-done | bytes 131104 | tf_op jit(solution)/shard_map/all_to_all | solution.py:87
  44.0 0.1 concatenate.50
  44.1 0.7 slice_maximum_fusion
  44.8 0.3 copy.146
  45.1 0.4 fusion.40
  45.5 0.2 fusion.8
  45.7 0.3 copy.149
  46.0 0.3 fusion.5
  46.3 0.1 copy.152
  46.4 0.1 reshape.384
  46.6 0.6 fusion.41
  47.2 0.1 add_bitcast_fusion
  47.3 1.1 dynamic_update_slice.4
  48.4 0.9 copy-done.1
  49.6 0.8 dynamic_slice.11
  50.5 0.4 select_reduce_fusion
  51.0 0.1 reshape.386
  51.1 0.1 copy.160
  51.2 0.1 copy.162
  51.4 119.2 %all-gather.5.cloned.1.call-done = f32[8,64,2880]{2,1,0:T(8,128)} async-done(((f32[1,64,2880]{2,1,0:T(8,128)}), f32[8,64,2880]{2,1,0:T(8,128)}) %all-gather.5.cloned.1.call-update) | async-done | bytes 5898256 | tf_op jit(solution)/shard_map/all_gather | solution.py:109
  170.5 3.1 reduce_sum.64
  173.6 0.2 multiply_reduce_fusion
  173.8 0.1 multiply_convert_fusion
  173.9 2.0 gather_fusion
  176.0 0.1 gather.18
  176.1 0.2 select_multiply_fusion
  176.4 60.1 %all_to_all.15 = bf16[64,10,360]{2,1,0:T(8,128)(2,1)S(1)} all-to-all(bf16[64,10,360]{2,1,0:T(8,128)(2,1)S(1)} %bitcast.62), channel_id=1, replica_groups=mesh['group'=64,'tp'=8] {'group'}, dimensions={0} | all-to-all | bytes 921600 | tf_op jit(solution)/shard_map/all_to_all | solution.py:139
  236.4 2.0 copy.165
  238.4 0.2 all-gather.9.cloned.1.call-start
  238.7 231.4 %all-gather.7.cloned.1.call-done = bf16[64,10,2880]{0,1,2:T(8,128)(2,1)} async-done(((bf16[64,10,360]{0,1,2:T(8,128)(2,1)}), bf16[64,10,2880]{0,1,2:T(8,128)(2,1)}) %all-gather.7.cloned.1.call-update) | async-done | bytes 3686416 | tf_op jit(solution)/shard_map/all_gather | solution.py:138
  470.0 17.0 %copy.166 = bf16[64,10,2880]{2,1,0:T(8,128)(2,1)} copy(bf16[64,10,2880]{0,1,2:T(8,128)(2,1)} %all-gather.7.cloned.1.call-done) | data formatting | bytes 7372800 | tf_op jit(solution)/shard_map/all_gather | solution.py:138
  487.0 7.8 %reshape.388 = bf16[640,2880]{1,0:T(8,128)(2,1)} reshape(bf16[64,10,2880]{2,1,0:T(8,128)(2,1)} %copy.166) | data formatting | bytes 7372800 | tf_op jit(solution)/shard_map/reshape | solution.py:145
  494.8 4.6 fusion
  499.4 0.9 fusion.14
  500.3 55.6 %all-gather.9.cloned.1.call-done = bf16[8,180,640]{2,1,0:T(8,128)(2,1)} async-done(((bf16[1,180,640]{2,1,0:T(8,128)(2,1)}), bf16[8,180,640]{2,1,0:T(8,128)(2,1)}) %all-gather.9.cloned.1.call-update) | async-done | bytes 1843216 | tf_op jit(solution)/shard_map/all_gather | solution.py:150
  555.9 2.6 reshape.423
  558.5 2.9 convolution_convert_fusion
  561.4 0.3 copy.167
  561.7 1.1 reshape.389
  562.8 16.0 %all-to-all-start.2 = ((bf16[64,10,360]{2,1,0:T(8,128)(2,1)}), bf16[64,10,360]{2,1,0:T(8,128)(2,1)S(1)}, u32[]{:S(2)}, u32[]{:S(2)}) async-start(bf16[64,10,360]{2,1,0:T(8,128)(2,1)} %reshape.389), calls=%async_computation.2 | async-start | bytes 1572864 | tf_op jit(solution)/shard_map/all_to_all | solution.py:155
  578.9 0.1 reshape.411
  579.0 1.9 gather_fusion.2
  580.9 0.1 reshape.414
  581.2 0.1 reshape.390
  581.3 0.1 copy.157
  581.6 42.0 %all-to-all-done.2 = bf16[64,10,360]{2,1,0:T(8,128)(2,1)S(1)} async-done(((bf16[64,10,360]{2,1,0:T(8,128)(2,1)}), bf16[64,10,360]{2,1,0:T(8,128)(2,1)S(1)}, u32[]{:S(2)}, u32[]{:S(2)}) %all-to-all-start.2) | async-done | bytes 460832 | tf_op jit(solution)/shard_map/all_to_all | solution.py:155
  623.7 0.2 convert.22
  624.0 1.0 gather_fusion.1
  625.0 0.1 gather.20
  625.1 0.4 multiply_reduce_fusion.1
  625.5 0.7 add_convert_fusion.1
  (53 shorter events, 1.6 us)
Async XLA Ops:
  6.5 40.0 %copy-start = (bf16[256,2880]{0,1:T(8,128)(2,1)S(1)}, bf16[256,2880]{0,1:T(8,128)(2,1)}, u32[]{:S(2)}) copy-start(bf16[256,2880]{0,1:T(8,128)(2,1)} %param.22) | copy-start | bytes 4423684
  6.5 24.3 %copy-start.5 = (f32[4]{0:T(128)S(1)}, f32[4]{0:T(128)}, u32[]{:S(2)}) copy-start(f32[4]{0:T(128)} %param.21) | copy-start | bytes 52
  6.5 37.4 %all-to-all-start = ((bf16[64,8,128]{2,1,0:T(8,128)(2,1)}), bf16[64,8,128]{2,1,0:T(8,128)(2,1)S(1)}, u32[]{:S(2)}, u32[]{:S(2)}) async-start(bf16[64,8,128]{2,1,0:T(8,128)(2,1)} %bitcast.69), calls=%async_computation | async-start | bytes 262144 | tf_op jit(solution)/shard_map/all_to_all | solution.py:87
  25.4 145.1 %all-gather.5.cloned.1.call-start = ((), (), s32[]{:S(2)}) async-start(), calls=%async_computation.3 | async-start | bytes 6782976 | tf_op jit(solution)/shard_map/all_gather | solution.py:109
  46.0 1.1 copy-start.2
  46.3 3.0 copy-start.3
  48.4 0.9 copy-start.1
  49.3 420.8 %all-gather.7.cloned.1.call-start = ((), (), s32[]{:S(2)}) async-start(), calls=%async_computation.4 | async-start | bytes 13271040 | tf_op jit(solution)/shard_map/all_gather | solution.py:138
  238.4 317.5 %all-gather.9.cloned.1.call-start = ((), (), s32[]{:S(2)}) async-start(), calls=%async_computation.5 | async-start | bytes 2119680 | tf_op jit(solution)/shard_map/all_gather | solution.py:150
  562.8 60.9 %all-to-all-start.2 = ((bf16[64,10,360]{2,1,0:T(8,128)(2,1)}), bf16[64,10,360]{2,1,0:T(8,128)(2,1)S(1)}, u32[]{:S(2)}, u32[]{:S(2)}) async-start(bf16[64,10,360]{2,1,0:T(8,128)(2,1)} %reshape.389), calls=%async_computation.2 | async-start | bytes 1572864 | tf_op jit(solution)/shard_map/all_to_all | solution.py:155
  579.0 2.5 copy-start.4
Sparse Core Ops, SparseCore 0:
  49.4 121.1 all-gather.4
  238.6 231.4 all-gather.6
  500.4 55.4 all-gather.8
